TPU v7x, 128 devices: a whole 4x4x4 slice. The times are simulated.
128 devices in a mesh: replica: 2 (over z_lo), shard: 64 (over x, y, z_hi, core).
Axes of the slice: x: 4, y: 4, z: 4 (z_hi: 2, z_lo: 2; z = z_hi * 2 + z_lo), core: 2. Of those that a mesh axis runs over, the one named last changes fastest.
Arguments:
- tokens: bfloat16 [131072, 960], P(('replica', 'shard')), may hold values from -6 to 6
- cotangent: bfloat16 [131072, 960], P(('replica', 'shard')), may hold values from -6 to 6
- query_weight: bfloat16 [960, 960], P('shard'), may hold values from -1 to 1
- key_weight: bfloat16 [960, 320], P('shard'), may hold values from -1 to 1
- value_weight: bfloat16 [960, 320], P('shard'), may hold values from -0.1875 to 0.1875
- w_gate: bfloat16 [960, 2560], P('shard'), may hold values from -0.1875 to 0.1875
- w_up: bfloat16 [960, 2560], P('shard'), may hold values from -0.1875 to 0.1875
- output_weight: bfloat16 [960, 960], P(None, 'shard'), may hold values from -0.75 to 0.75
- w_down: bfloat16 [2560, 960], P(None, 'shard'), may hold values from -0.125 to 0.125
- norm_attn: bfloat16 [960], P('shard'), may hold values from 0.5 to 1.5
- norm_ffn: bfloat16 [960], P('shard'), may hold values from 0.5 to 1.5
Outputs:
- output: bfloat16 [131072, 960], P(('replica', 'shard'))
- grad_tokens: float32 [131072, 960], P(('replica', 'shard'))
- grad_query: float32 [960, 960], P('shard')
- grad_key: float32 [960, 320], P('shard')
- grad_value: float32 [960, 320], P('shard')
- grad_gate: float32 [960, 2560], P('shard')
- grad_up: float32 [960, 2560], P('shard')
- grad_out: float32 [960, 960], P(None, 'shard')
- grad_down: float32 [2560, 960], P(None, 'shard')
- grad_norm_attn: float32 [960], P('shard')
- grad_norm_ffn: float32 [960], P('shard')
All inputs are finite; a program needn't handle non-finite values.
Results may differ from a plain program's by a relative error of at most 0.018.
The roundings to bfloat16 on the way count: a program that leaves them out, or rounds other values in their place, can miss the bound.
Values may be sent and summed in bfloat16 or wider, within the bound.
A program may use at most 256 MiB of HBM per device.

v0:
```python
import math
import jax
import jax.numpy as jnp
from jax import lax
from jax.sharding import PartitionSpec as P

HQ = 15
KEY_VALUE_HEADS = 5
HEAD_SIZE = 64
SEQUENCE_TOKENS = 512
QUERY_PER_KEY = 3
EPSILON = 1e-05


def gather_turned(arrays, axis, dims):
    turned = [jnp.moveaxis(a, dim, 0) for a, dim in zip(arrays, dims)]
    both = jnp.concatenate([t.reshape(len(t), -1) for t in turned], axis=1)
    whole, at, finished = (lax.all_gather(both, axis, axis=0, tiled=True), 0, [])
    for t, dim in zip(turned, dims):
        section = whole[:, at : at + t[0].size].reshape(-1, *t.shape[1:])
        finished.append(jnp.moveaxis(section, 0, dim))
        at += t[0].size
    return tuple(finished)


def packed_total(arrays, axis):
    vector, at, finished = (jnp.concatenate([a.reshape(-1) for a in arrays]), 0, [])
    so_far = lax.psum(vector, axis)
    for a in arrays:
        finished.append(so_far[at : at + a.size].reshape(a.shape))
        at += a.size
    return tuple(finished)


def swap_half_pairs(values):
    middle = values.shape[-1] // 2
    return jnp.concatenate([-values[..., middle:], values[..., :middle]], axis=-1)


def rope_tables():
    half_dim = HEAD_SIZE // 2
    rates = jnp.exp(
        jnp.arange(half_dim, dtype=jnp.float32) * (-2.0 * math.log(10000.0) / HEAD_SIZE)
    )
    angles = jnp.arange(SEQUENCE_TOKENS, dtype=jnp.float32)[:, None] * rates[None, :]
    angles = jnp.concatenate([angles, angles], axis=-1)
    return (jnp.cos(angles), jnp.sin(angles))


def causal_mask():
    row_ids = lax.broadcasted_iota(jnp.int32, (SEQUENCE_TOKENS, SEQUENCE_TOKENS), 0)
    col_ids = lax.broadcasted_iota(jnp.int32, (SEQUENCE_TOKENS, SEQUENCE_TOKENS), 1)
    return col_ids <= row_ids


def score_block(queries, key_block):
    scores = jnp.einsum(
        "qkgd,tkd->kgqt", queries, key_block, preferred_element_type=jnp.float32
    ) * (1.0 / math.sqrt(HEAD_SIZE))
    return jnp.where(causal_mask(), scores, -1e30)


def attend_forward(packed_in):
    queries, key_block, values = packed_in
    scores = score_block(queries, key_block)
    row_top = jnp.max(scores, axis=-1)
    log_total = row_top + jnp.log(jnp.sum(jnp.exp(scores - row_top[..., None]), axis=-1))
    soft_low = jnp.exp(scores - log_total[..., None]).astype(jnp.bfloat16)
    heads_out = jnp.einsum(
        "kgqt,tkd->qkgd", soft_low, values, preferred_element_type=jnp.float32
    ).astype(jnp.bfloat16)
    return (heads_out, log_total)


def attend_backward(packed_in):
    queries, key_block, values, heads_out, log_total, head_output_gradient = packed_in
    scores = score_block(queries, key_block)
    soft_full = jnp.exp(scores - log_total[..., None])
    soft_low = soft_full.astype(jnp.bfloat16)
    value_rows_gradient = jnp.einsum(
        "kgqt,qkgd->tkd", soft_low, head_output_gradient, preferred_element_type=jnp.float32
    )
    grad_soft = jnp.einsum(
        "qkgd,tkd->kgqt", head_output_gradient, values, preferred_element_type=jnp.float32
    )
    offset = jnp.transpose(
        jnp.sum(head_output_gradient.astype(jnp.float32) * heads_out.astype(jnp.float32), axis=-1),
        (1, 2, 0),
    )
    grad_scores = (soft_full * (grad_soft - offset[..., None])).astype(jnp.bfloat16)
    scale = 1.0 / math.sqrt(HEAD_SIZE)
    grad_queries = (
        jnp.einsum("kgqt,tkd->qkgd", grad_scores, key_block, preferred_element_type=jnp.float32)
        * scale
    )
    key_rows_gradient = (
        jnp.einsum("kgqt,qkgd->tkd", grad_scores, queries, preferred_element_type=jnp.float32)
        * scale
    )
    return (grad_queries, key_rows_gradient, value_rows_gradient)


def tdot(left, right):
    return lax.dot_general(
        left, right, (((0,), (0,)), ((), ())), preferred_element_type=jnp.float32
    )


def contract_product(left, weight):
    return lax.dot_general(
        left, weight, (((1,), (1,)), ((), ())), preferred_element_type=jnp.float32
    )


def forward(tokens, weights):
    (
        query_weight,
        key_weight,
        value_weight,
        w_gate,
        w_up,
        output_weight,
        w_down,
        norm_attn,
        norm_ffn,
    ) = weights
    count_of_rows = tokens.shape[0]
    sequence_count = count_of_rows // SEQUENCE_TOKENS
    inputs = tokens.astype(jnp.float32)
    recip_attn = lax.rsqrt(jnp.mean(inputs * inputs, axis=-1, keepdims=True) + EPSILON)
    attention_normalized = (inputs * recip_attn * norm_attn.astype(jnp.float32)).astype(
        jnp.bfloat16
    )
    cosine_table, sine_table = rope_tables()
    rotated_query = jnp.dot(
        attention_normalized, query_weight, preferred_element_type=jnp.float32
    ).reshape(sequence_count, SEQUENCE_TOKENS, KEY_VALUE_HEADS, QUERY_PER_KEY, HEAD_SIZE)
    rotated_query = (
        rotated_query * cosine_table[:, None, None, :]
        + swap_half_pairs(rotated_query) * sine_table[:, None, None, :]
    ).astype(jnp.bfloat16)
    rotated_key = jnp.dot(
        attention_normalized, key_weight, preferred_element_type=jnp.float32
    ).reshape(sequence_count, SEQUENCE_TOKENS, KEY_VALUE_HEADS, HEAD_SIZE)
    rotated_key = (
        rotated_key * cosine_table[:, None, :]
        + swap_half_pairs(rotated_key) * sine_table[:, None, :]
    ).astype(jnp.bfloat16)
    value_per_head = (
        jnp.dot(attention_normalized, value_weight, preferred_element_type=jnp.float32)
        .astype(jnp.bfloat16)
        .reshape(sequence_count, SEQUENCE_TOKENS, KEY_VALUE_HEADS, HEAD_SIZE)
    )
    heads_out, log_total = lax.map(attend_forward, (rotated_query, rotated_key, value_per_head))
    attended = heads_out.reshape(count_of_rows, HQ * HEAD_SIZE)
    hidden = inputs + jnp.dot(attended, output_weight, preferred_element_type=jnp.float32)
    recip_ffn = lax.rsqrt(jnp.mean(hidden * hidden, axis=-1, keepdims=True) + EPSILON)
    normed_ffn = (hidden * recip_ffn * norm_ffn.astype(jnp.float32)).astype(jnp.bfloat16)
    gate_pre = jnp.dot(normed_ffn, w_gate, preferred_element_type=jnp.float32)
    upward = jnp.dot(normed_ffn, w_up, preferred_element_type=jnp.float32)
    sigmoid_gate = jax.nn.sigmoid(gate_pre)
    activated = (gate_pre * sigmoid_gate * upward).astype(jnp.bfloat16)
    output = (hidden + jnp.dot(activated, w_down, preferred_element_type=jnp.float32)).astype(
        jnp.bfloat16
    )
    saved = (
        inputs,
        recip_attn,
        attention_normalized,
        rotated_query,
        rotated_key,
        value_per_head,
        heads_out,
        log_total,
        hidden,
        recip_ffn,
        normed_ffn,
        gate_pre,
        upward,
        sigmoid_gate,
        activated,
    )
    return (output, saved)


def ffn_backward(saved, cotangent, weights):
    (
        query_weight,
        key_weight,
        value_weight,
        w_gate,
        w_up,
        output_weight,
        w_down,
        norm_attn,
        norm_ffn,
    ) = weights
    (
        inputs,
        recip_attn,
        attention_normalized,
        rotated_query,
        rotated_key,
        value_per_head,
        heads_out,
        log_total,
        hidden,
        recip_ffn,
        normed_ffn,
        gate_pre,
        upward,
        sigmoid_gate,
        activated,
    ) = saved
    grad_w_down = tdot(activated, cotangent)
    grad_act = contract_product(cotangent, w_down)
    gate_slope = sigmoid_gate * (1.0 + gate_pre * (1.0 - sigmoid_gate))
    grad_gate_low = (grad_act * upward * gate_slope).astype(jnp.bfloat16)
    grad_upward_low = (grad_act * gate_pre * sigmoid_gate).astype(jnp.bfloat16)
    grad_w_gate = tdot(normed_ffn, grad_gate_low)
    grad_w_up = tdot(normed_ffn, grad_upward_low)
    grad_normed = contract_product(grad_gate_low, w_gate) + contract_product(grad_upward_low, w_up)
    grad_norm_ffn = jnp.sum(grad_normed * hidden * recip_ffn, axis=0)
    scaled = grad_normed * norm_ffn.astype(jnp.float32)
    grad_hidden = (
        cotangent.astype(jnp.float32)
        + recip_ffn * scaled
        - hidden * recip_ffn**3 * jnp.mean(scaled * hidden, axis=-1, keepdims=True)
    )
    return (grad_hidden, (grad_w_gate, grad_w_up, grad_w_down, grad_norm_ffn))


def attn_backward(saved, grad_hidden, weights):
    (
        query_weight,
        key_weight,
        value_weight,
        w_gate,
        w_up,
        output_weight,
        w_down,
        norm_attn,
        norm_ffn,
    ) = weights
    (
        inputs,
        recip_attn,
        attention_normalized,
        rotated_query,
        rotated_key,
        value_per_head,
        heads_out,
        log_total,
        hidden,
        recip_ffn,
        normed_ffn,
        gate_pre,
        upward,
        sigmoid_gate,
        activated,
    ) = saved
    count_of_rows = inputs.shape[0]
    sequence_count = count_of_rows // SEQUENCE_TOKENS
    cosine_table, sine_table = rope_tables()
    hidden_gradient_narrow = grad_hidden.astype(jnp.bfloat16)
    attended = heads_out.reshape(count_of_rows, HQ * HEAD_SIZE)
    grad_w_out = tdot(attended, hidden_gradient_narrow)
    head_output_gradient = (
        contract_product(hidden_gradient_narrow, output_weight)
        .astype(jnp.bfloat16)
        .reshape(sequence_count, SEQUENCE_TOKENS, KEY_VALUE_HEADS, QUERY_PER_KEY, HEAD_SIZE)
    )
    grad_queries, key_rows_gradient, value_rows_gradient = lax.map(
        attend_backward,
        (rotated_query, rotated_key, value_per_head, heads_out, log_total, head_output_gradient),
    )
    grad_queries = (
        (
            grad_queries * cosine_table[:, None, None, :]
            - swap_half_pairs(grad_queries) * sine_table[:, None, None, :]
        )
        .astype(jnp.bfloat16)
        .reshape(count_of_rows, HQ * HEAD_SIZE)
    )
    key_rows_gradient = (
        (
            key_rows_gradient * cosine_table[:, None, :]
            - swap_half_pairs(key_rows_gradient) * sine_table[:, None, :]
        )
        .astype(jnp.bfloat16)
        .reshape(count_of_rows, KEY_VALUE_HEADS * HEAD_SIZE)
    )
    value_rows_gradient = value_rows_gradient.astype(jnp.bfloat16).reshape(
        count_of_rows, KEY_VALUE_HEADS * HEAD_SIZE
    )
    grad_w_query = tdot(attention_normalized, grad_queries)
    grad_w_key = tdot(attention_normalized, key_rows_gradient)
    grad_w_value = tdot(attention_normalized, value_rows_gradient)
    grad_normed_attn = (
        contract_product(grad_queries, query_weight)
        + contract_product(key_rows_gradient, key_weight)
        + contract_product(value_rows_gradient, value_weight)
    )
    grad_norm_attn = jnp.sum(grad_normed_attn * inputs * recip_attn, axis=0)
    scaled_attn = grad_normed_attn * norm_attn.astype(jnp.float32)
    grad_tokens = (
        grad_hidden
        + recip_attn * scaled_attn
        - inputs * recip_attn**3 * jnp.mean(scaled_attn * inputs, axis=-1, keepdims=True)
    )
    return (grad_tokens, (grad_w_query, grad_w_key, grad_w_value, grad_w_out, grad_norm_attn))


def shards(
    tokens,
    cotangent,
    query_weight,
    key_weight,
    value_weight,
    w_gate,
    w_up,
    output_weight,
    w_down,
    norm_attn,
    norm_ffn,
):
    gathered = gather_turned(
        (
            query_weight,
            key_weight,
            value_weight,
            w_gate,
            w_up,
            output_weight,
            w_down,
            norm_attn,
            norm_ffn,
        ),
        "shard",
        (0, 0, 0, 0, 0, 1, 1, 0, 0),
    )
    output, saved = forward(tokens, gathered)
    back_weights = gather_turned(
        (
            query_weight,
            key_weight,
            value_weight,
            w_gate,
            w_up,
            output_weight,
            w_down,
            norm_attn,
            norm_ffn,
        ),
        "shard",
        (0, 0, 0, 0, 0, 1, 1, 0, 0),
    )
    grad_hidden, ffn_grads = ffn_backward(saved, cotangent, back_weights)
    g_gate, g_up, g_down, g_norm_ffn = ffn_grads
    grad_tokens, attn_grads = attn_backward(saved, grad_hidden, back_weights)
    g_query, g_key, g_value, g_out, g_norm_attn = attn_grads
    owned = (
        lax.psum_scatter(g_query, "shard", scatter_dimension=0, tiled=True),
        lax.psum_scatter(g_key, "shard", scatter_dimension=0, tiled=True),
        lax.psum_scatter(g_value, "shard", scatter_dimension=0, tiled=True),
        lax.psum_scatter(g_gate, "shard", scatter_dimension=0, tiled=True),
        lax.psum_scatter(g_up, "shard", scatter_dimension=0, tiled=True),
        lax.psum_scatter(g_out, "shard", scatter_dimension=1, tiled=True),
        lax.psum_scatter(g_down, "shard", scatter_dimension=1, tiled=True),
        lax.psum_scatter(g_norm_attn, "shard", scatter_dimension=0, tiled=True),
        lax.psum_scatter(g_norm_ffn, "shard", scatter_dimension=0, tiled=True),
    )
    o_query, o_key, o_value, o_gate, o_up, o_out, o_down, o_norm_attn, o_norm_ffn = owned
    shares = tuple(
        (
            part.astype(jnp.float32)
            for part in packed_total(
                (
                    o_query.astype(jnp.bfloat16),
                    o_key.astype(jnp.bfloat16),
                    o_value.astype(jnp.bfloat16),
                    o_gate.astype(jnp.bfloat16),
                    o_up.astype(jnp.bfloat16),
                    o_out.astype(jnp.bfloat16),
                    o_down.astype(jnp.bfloat16),
                    o_norm_attn.astype(jnp.bfloat16),
                    o_norm_ffn.astype(jnp.bfloat16),
                ),
                "replica",
            )
        )
    )
    s_query, s_key, s_value, s_gate, s_up, s_out, s_down, s_norm_attn, s_norm_ffn = shares
    return (
        output,
        grad_tokens,
        s_query,
        s_key,
        s_value,
        s_gate,
        s_up,
        s_out,
        s_down,
        s_norm_attn,
        s_norm_ffn,
    )


def solution(mesh):
    in_specs = (
        P(("replica", "shard"), None),
        P(("replica", "shard"), None),
        P("shard", None),
        P("shard", None),
        P("shard", None),
        P("shard", None),
        P("shard", None),
        P(None, "shard"),
        P(None, "shard"),
        P("shard"),
        P("shard"),
    )
    out_specs = (
        P(("replica", "shard"), None),
        P(("replica", "shard"), None),
        P("shard", None),
        P("shard", None),
        P("shard", None),
        P("shard", None),
        P("shard", None),
        P(None, "shard"),
        P(None, "shard"),
        P("shard"),
        P("shard"),
    )
    return jax.shard_map(shards, mesh=mesh, in_specs=in_specs, out_specs=out_specs, check_vma=False)
```

profile of v0, /device:TPU:1, one launch (start us, length us, event | category | flops | bytes accessed | tf_op | source)
XLA Modules:
  0.0 1250.7 jit_solution(898325108105369608)
XLA Ops:
  16.5 118.3 %all-gather.3.cloned.1.call-done = bf16[64,15,10242]{2,1,0:T(8,128)(2,1)} async-done(((bf16[1,15,10242]{2,1,0:T(8,128)(2,1)}), bf16[64,15,10242]{2,1,0:T(8,128)(2,1)}) %all-gather.3.cloned.1.call-update) | async-done | bytes 19664656 | tf_op jit(solution)/shard_map/all_gather | solution.py:18
  134.8 20.1 %reshape.306 = bf16[960,10242]{1,0:T(8,128)(2,1)} reshape(bf16[64,15,10242]{2,1,0:T(8,128)(2,1)} %all-gather.3.cloned.1.call-done) | data formatting | bytes 39329280
  162.1 5.8 fusion.99
  172.2 6.4 reshape.282
  184.9 50.4 %while.26 = (s32[]{:T(128)}, bf16[2,512,5,3,64]{1,4,3,2,0:T(8,128)(2,1)}, f32[2,5,3,512]{3,2,1,0:T(4,128)}, bf16[2,512,5,64]{1,3,2,0:T(8,128)(2,1)S(1)}, bf16[2,...) while((s32[]{:T(128)}, bf16[2,512,5,3,64]{1,4,3,2,0:T(8,128)(2,1)}, ...), condition=%wide.region_4.5_spmd, body=%wide.region_1.4_spmd.sunk | while | flops 1050632704 | bytes 67375304 | solution.py:154
  185.0 6.9 fusion.180
  191.9 8.9 exponential_reduce_fusion.2
  200.9 7.8 fusion.181
  210.0 6.9 fusion.180
  217.0 8.9 exponential_reduce_fusion.2
  225.9 7.8 fusion.181
  239.6 4.6 multiply_reduce_fusion.2
  246.6 11.7 fusion.78
  258.3 10.7 fusion.68
  269.0 19.1 %fusion.65 = (bf16[1024,2560]{1,0:T(8,128)(2,1)}, bf16[1024,2560]{1,0:T(8,128)(2,1)}, bf16[1024,2560]{1,0:T(8,128)(2,1)}) fusion(f32[2560,1024]{0,1:T(8,128)} %fusion.68, f32[1024,2560]{1,0:T(8,128)} %fusion.78, bf16[1024,960]{0,1:T(8,128)(2,1)} %copy-done.23, bf16[960,10242]{1,0:T(8,128)(2,1)} %reshape.306), kind=kOutput, calls=%fused_computation.68 | convolution fusion | flops 5075107840 | bytes 43581440 | tf_op jit(solution)/shard_map/dot_general | solution.py:160
  288.1 9.1 fusion.72
  297.3 9.1 multiply_reduce_fusion
  308.0 4.2 fusion.107
  312.2 5.7 convolution_convert_fusion
  318.0 6.2 reshape.284
  327.4 59.5 %while.27 = (s32[]{:T(128)}, f32[2,512,5,3,64]{1,4,3,2,0:T(8,128)}, f32[2,512,5,64]{1,3,2,0:T(8,128)}, bf16[2,512,5,64]{1,3,2,0:T(8,128)(2,1)}, bf16[2,512,5,64]...) while((s32[]{:T(128)}, f32[2,512,5,3,64]{1,4,3,2,0:T(8,128)}, ...), condition=%wide.region_9.10_spmd, body=%wide.region_7.9_spmd.sunk | while | flops 2558779904 | bytes 186770704 | solution.py:273
  331.6 5.4 copy-done
  337.0 5.6 fusion.196
  342.6 8.6 fusion.194
  361.3 5.4 copy-done
  366.7 5.6 fusion.196
  372.3 8.6 fusion.194
  393.5 4.6 fusion.110
  402.7 4.2 fusion.122
  406.9 5.8 fusion.97
  412.7 8.0 fusion.136
  420.7 7.7 fusion.137
  428.5 9.0 add_convert_fusion
  437.4 7.8 fusion.138
  448.3 463.7 %fusion.127 = (f32[16,960]{1,0:T(8,128)S(1)}, f32[16,320]{1,0:T(8,128)S(1)}, f32[16,320]{1,0:T(8,128)S(1)}, f32[16,2560]{1,0:T(8,128)S(1)}, f32[16,2560]{1,0:T(8...) fusion(f32[960,960]{1,0:T(8,128)} %fusion.122, f32[960,320]{1,0:T(8,128)} %fusion.120, ...), kind=kCustom, calls=%all-reduce-scatter.7 | all-reduce-scatter fusion | flops 10485761 | bytes 39977472
  913.4 8.0 collective-permute-start.10
  926.5 7.2 fusion.87
  937.0 164.9 %all-reduce.16 = (bf16[960]{0:T(1024)(128)(2,1)S(1)}, bf16[960]{0:T(1024)(128)(2,1)S(1)}) all-reduce(f32[960]{0:T(1024)S(1)} %get-tuple-element.177, f32[960]{0:T(1024)S(1)} %copy-done.38), channel_id=9, replica_groups=mesh['replica'=2,'shard'=64] {'shard'}, use_global_device_ids=true, to_apply=%region_19.20.clone | all-reduce | flops 1920 | bytes 11520
  1125.2 3.9 collective-permute-start.20
  1130.4 4.5 collective-permute-start.25
  1138.1 4.4 collective-permute-start.24
  1153.5 5.0 collective-permute-start.16
  1158.5 6.7 collective-permute-start.19
  1169.9 5.8 collective-permute-start.12
  1175.7 9.9 collective-permute-start.15
  1190.7 8.3 concatenate.45
  1199.0 6.2 fusion.84
  1205.2 27.0 %all-reduce.20.cloned.1.call-done = bf16[153630]{0:T(1024)(128)(2,1)} async-done(((bf16[153630]{0:T(1024)(128)(2,1)}), bf16[153630]{0:T(1024)(128)(2,1)}) %all-reduce.20.cloned.1.call-update) | async-done | bytes 307276 | tf_op jit(solution)/shard_map/psum | solution.py:28
  (281 shorter events, 143.0 us)
Async XLA Ops:
  7.2 127.6 %all-gather.3.cloned.1.call-start = ((), (), s32[]{:S(2)}) async-start(), calls=%async_computation.1 | async-start | bytes 21565440 | tf_op jit(solution)/shard_map/all_gather | solution.py:18
  10.7 1221.5 %all-reduce.20.cloned.1.call-start = ((), (), s32[]{:S(2)}) async-start(), calls=%async_computation | async-start | bytes 618496 | tf_op jit(solution)/shard_map/psum | solution.py:28
  13.8 168.7 %copy-start.16 = (f32[512,64]{0,1:T(8,128)}, f32[512,64]{0,1:T(8,128)S(1)}, u32[]{:S(2)}) copy-start(f32[512,64]{0,1:T(8,128)S(1)} %get-tuple-element.266) | copy-start | bytes 393220
  13.8 168.7 %copy-start.18 = (f32[512,64]{0,1:T(8,128)}, f32[512,64]{0,1:T(8,128)S(1)}, u32[]{:S(2)}) copy-start(f32[512,64]{0,1:T(8,128)S(1)} %get-tuple-element.267) | copy-start | bytes 393220
  16.5 145.6 %copy-start.35 = (f32[1024]{0:T(1024)}, f32[1024]{0:T(1024)S(1)}, u32[]{:S(2)}) copy-start(f32[1024]{0:T(1024)S(1)} %get-tuple-element.275) | copy-start | bytes 12292
  16.5 139.8 %copy-start.4 = (bf16[1024,960]{0,1:T(8,128)(2,1)S(1)}, bf16[1024,960]{0,1:T(8,128)(2,1)}, u32[]{:S(2)}) copy-start(bf16[1024,960]{0,1:T(8,128)(2,1)} %param.15) | copy-start | bytes 5898244
  246.6 11.7 copy-start.23
  246.6 11.7 copy-start.20
  297.3 9.2 copy-start.21
  318.0 9.4 copy-start.31
  327.4 61.2 %copy-start.17 = (f32[512,64]{0,1:T(8,128)S(1)}, f32[512,64]{0,1:T(8,128)}, u32[]{:S(2)}) copy-start(f32[512,64]{0,1:T(8,128)} %copy-done.16) | copy-start | bytes 393220
  327.4 61.2 %copy-start.19 = (f32[512,64]{0,1:T(8,128)S(1)}, f32[512,64]{0,1:T(8,128)}, u32[]{:S(2)}) copy-start(f32[512,64]{0,1:T(8,128)} %copy-done.18) | copy-start | bytes 393220
  402.2 10.5 slice-start.4
  402.7 10.0 slice-start.5
  406.9 13.8 %slice-start.2 = ((s8[5242880]{0:T(1024)(128)(4,1)}), s8[4194304]{0:T(1024)(128)(4,1)S(1)}, s32[]{:S(2)}) async-start(s8[5242880]{0:T(1024)(128)(4,1)} %bitcast.280), calls=%async_computation.4 | async-start | bytes 8388608
  412.7 15.7 %slice-start = ((s8[5242880]{0:T(1024)(128)(4,1)}), s8[4194304]{0:T(1024)(128)(4,1)S(1)}, s32[]{:S(2)}) async-start(s8[5242880]{0:T(1024)(128)(4,1)} %bitcast.278), calls=%async_computation.2 | async-start | bytes 8388608
  912.1 24.9 %copy-start.38 = (f32[960]{0:T(1024)S(1)}, f32[960]{0:T(1024)}, u32[]{:S(2)}) copy-start(f32[960]{0:T(1024)} %get-tuple-element.175) | copy-start | bytes 11524
  912.1 193.5 %collective-permute-start.9 = (bf16[16,320]{1,0:T(8,128)(2,1)S(1)}, bf16[16,320]{1,0:T(8,128)(2,1)S(1)}, u32[]{:S(2)}, u32[]{:S(2)}) collective-permute-start(bf16[16,320]{1,0:T(8,128)(2,1)S(1)} %convert.74), channel_id=1, source_target_pairs={{0,2},{1,3},{2,4},{3,5},{4,6},{5,7},{6,8},{7,9},{8,10},{9,11},{10,... | collective-permute-start | bytes 30728
  913.4 194.2 %collective-permute-start.10 = (bf16[16,320]{1,0:T(8,128)(2,1)S(1)}, bf16[16,320]{1,0:T(8,128)(2,1)S(1)}, u32[]{:S(2)}, u32[]{:S(2)}) collective-permute-start(bf16[16,320]{1,0:T(8,128)(2,1)S(1)} %convert.74), channel_id=1, source_target_pairs={{0,3},{1,4},{2,5},{3,6},{4,7},{5,8},{6,9},{7,10},{8,11},{9,12},{10... | collective-permute-start | bytes 30728
  921.4 187.5 %collective-permute-start.8 = (bf16[16,320]{1,0:T(8,128)(2,1)S(1)}, bf16[16,320]{1,0:T(8,128)(2,1)S(1)}, u32[]{:S(2)}, u32[]{:S(2)}) collective-permute-start(bf16[16,320]{1,0:T(8,128)(2,1)S(1)} %convert.74), channel_id=1, source_target_pairs={{0,1},{1,2},{2,3},{3,4},{4,5},{5,6},{6,7},{7,8},{8,9},{9,10},{10,1... | collective-permute-start | bytes 30728
  923.3 181.0 %collective-permute-start.11 = (bf16[15,320]{1,0:T(8,128)(2,1)S(1)}, bf16[15,320]{1,0:T(8,128)(2,1)S(1)}, u32[]{:S(2)}, u32[]{:S(2)}) collective-permute-start(bf16[15,320]{1,0:T(8,128)(2,1)S(1)} %slice.153), channel_id=1, source_target_pairs={{0,4},{1,5},{2,6},{3,7},{4,8},{5,9},{6,10},{7,11},{8,12},{9,13},{1... | collective-permute-start | bytes 28808
  1103.0 11.5 collective-permute-start.5
  1104.3 13.9 %collective-permute-start.6 = (bf16[16,320]{1,0:T(8,128)(2,1)S(1)}, bf16[16,320]{1,0:T(8,128)(2,1)S(1)}, u32[]{:S(2)}, u32[]{:S(2)}) collective-permute-start(bf16[16,320]{1,0:T(8,128)(2,1)S(1)} %convert.75), channel_id=1, source_target_pairs={{0,3},{1,4},{2,5},{3,6},{4,7},{5,8},{6,9},{7,10},{8,11},{9,12},{10... | collective-permute-start | bytes 30728
  1105.7 13.9 %collective-permute-start.4 = (bf16[16,320]{1,0:T(8,128)(2,1)S(1)}, bf16[16,320]{1,0:T(8,128)(2,1)S(1)}, u32[]{:S(2)}, u32[]{:S(2)}) collective-permute-start(bf16[16,320]{1,0:T(8,128)(2,1)S(1)} %convert.75), channel_id=1, source_target_pairs={{0,1},{1,2},{2,3},{3,4},{4,5},{5,6},{6,7},{7,8},{8,9},{9,10},{10,1... | collective-permute-start | bytes 30728
  1107.6 3.3 collective-permute-start.7
  1108.9 16.3 %collective-permute-start.1 = (bf16[16,960]{1,0:T(8,128)(2,1)S(1)}, bf16[16,960]{1,0:T(8,128)(2,1)S(1)}, u32[]{:S(2)}, u32[]{:S(2)}) collective-permute-start(bf16[16,960]{1,0:T(8,128)(2,1)S(1)} %convert.73), channel_id=1, source_target_pairs={{0,2},{1,3},{2,4},{3,5},{4,6},{5,7},{6,8},{7,9},{8,10},{9,11},{10,... | collective-permute-start | bytes 92168
  1110.9 18.2 %collective-permute-start.2 = (bf16[16,960]{1,0:T(8,128)(2,1)S(1)}, bf16[16,960]{1,0:T(8,128)(2,1)S(1)}, u32[]{:S(2)}, u32[]{:S(2)}) collective-permute-start(bf16[16,960]{1,0:T(8,128)(2,1)S(1)} %convert.73), channel_id=1, source_target_pairs={{0,3},{1,4},{2,5},{3,6},{4,7},{5,8},{6,9},{7,10},{8,11},{9,12},{10... | collective-permute-start | bytes 92168
  1114.6 15.8 %collective-permute-start = (bf16[16,960]{1,0:T(8,128)(2,1)S(1)}, bf16[16,960]{1,0:T(8,128)(2,1)S(1)}, u32[]{:S(2)}, u32[]{:S(2)}) collective-permute-start(bf16[16,960]{1,0:T(8,128)(2,1)S(1)} %convert.73), channel_id=1, source_target_pairs={{0,1},{1,2},{2,3},{3,4},{4,5},{5,6},{6,7},{7,8},{8,9},{9,10},{10,1... | collective-permute-start | bytes 92168
  1118.2 5.7 collective-permute-start.3
  1119.5 18.6 %collective-permute-start.21 = (bf16[960,16]{0,1:T(8,128)(2,1)S(1)}, bf16[960,16]{0,1:T(8,128)(2,1)S(1)}, u32[]{:S(2)}, u32[]{:S(2)}) collective-permute-start(bf16[960,16]{0,1:T(8,128)(2,1)S(1)} %convert.72), channel_id=1, source_target_pairs={{0,2},{1,3},{2,4},{3,5},{4,6},{5,7},{6,8},{7,9},{8,10},{9,11},{10,... | collective-permute-start | bytes 92168
  1123.9 18.6 %collective-permute-start.22 = (bf16[960,16]{0,1:T(8,128)(2,1)S(1)}, bf16[960,16]{0,1:T(8,128)(2,1)S(1)}, u32[]{:S(2)}, u32[]{:S(2)}) collective-permute-start(bf16[960,16]{0,1:T(8,128)(2,1)S(1)} %convert.72), channel_id=1, source_target_pairs={{0,3},{1,4},{2,5},{3,6},{4,7},{5,8},{6,9},{7,10},{8,11},{9,12},{10... | collective-permute-start | bytes 92168
  1125.2 20.7 %collective-permute-start.20 = (bf16[960,16]{0,1:T(8,128)(2,1)S(1)}, bf16[960,16]{0,1:T(8,128)(2,1)}, u32[]{:S(2)}, u32[]{:S(2)}) collective-permute-start(bf16[960,16]{0,1:T(8,128)(2,1)S(1)} %convert.72), channel_id=1, source_target_pairs={{0,1},{1,2},{2,3},{3,4},{4,5},{5,6},{6,7},{7,8},{8,9},{9,10},{10,1... | collective-permute-start | bytes 92168
  1129.1 6.5 collective-permute-start.23
  1130.4 23.1 %collective-permute-start.25 = (bf16[2560,16]{0,1:T(8,128)(2,1)S(1)}, bf16[2560,16]{0,1:T(8,128)(2,1)S(1)}, u32[]{:S(2)}, u32[]{:S(2)}) collective-permute-start(bf16[2560,16]{0,1:T(8,128)(2,1)S(1)} %convert.69), channel_id=1, source_target_pairs={{0,2},{1,3},{2,4},{3,5},{4,6},{5,7},{6,8},{7,9},{8,10},{9,11},{10,... | collective-permute-start | bytes 245768
  1135.6 22.9 %collective-permute-start.26 = (bf16[2560,16]{0,1:T(8,128)(2,1)S(1)}, bf16[2560,16]{0,1:T(8,128)(2,1)S(1)}, u32[]{:S(2)}, u32[]{:S(2)}) collective-permute-start(bf16[2560,16]{0,1:T(8,128)(2,1)S(1)} %convert.69), channel_id=1, source_target_pairs={{0,3},{1,4},{2,5},{3,6},{4,7},{5,8},{6,9},{7,10},{8,11},{9,12},{10... | collective-permute-start | bytes 245768
  1138.1 27.0 %collective-permute-start.24 = (bf16[2560,16]{0,1:T(8,128)(2,1)S(1)}, bf16[2560,16]{0,1:T(8,128)(2,1)S(1)}, u32[]{:S(2)}, u32[]{:S(2)}) collective-permute-start(bf16[2560,16]{0,1:T(8,128)(2,1)S(1)} %convert.69), channel_id=1, source_target_pairs={{0,1},{1,2},{2,3},{3,4},{4,5},{5,6},{6,7},{7,8},{8,9},{9,10},{10,1... | collective-permute-start | bytes 245768
  1142.5 9.2 collective-permute-start.27
  1145.9 24.0 %collective-permute-start.17 = (bf16[16,2560]{1,0:T(8,128)(2,1)}, bf16[16,2560]{1,0:T(8,128)(2,1)S(1)}, u32[]{:S(2)}, u32[]{:S(2)}) collective-permute-start(bf16[16,2560]{1,0:T(8,128)(2,1)} %convert.70), channel_id=1, source_target_pairs={{0,2},{1,3},{2,4},{3,5},{4,6},{5,7},{6,8},{7,9},{8,10},{9,11},{10,... | collective-permute-start | bytes 245768
  1151.1 39.6 %copy-start.32 = (bf16[4800]{0:T(1024)(128)(2,1)S(1)}, bf16[4800]{0:T(1024)(128)(2,1)}, u32[]{:S(2)}) copy-start(bf16[4800]{0:T(1024)(128)(2,1)} %reshape.289) | copy-start | bytes 28804
  1151.1 39.6 %copy-start.39 = (bf16[15]{0:T(256)(128)(2,1)S(1)}, bf16[15]{0:T(256)(128)(2,1)}, u32[]{:S(2)}) copy-start(bf16[15]{0:T(256)(128)(2,1)} %dynamic-slice.56) | copy-start | bytes 94
  1151.1 39.6 %copy-start.40 = (bf16[15]{0:T(256)(128)(2,1)S(1)}, bf16[15]{0:T(256)(128)(2,1)}, u32[]{:S(2)}) copy-start(bf16[15]{0:T(256)(128)(2,1)} %dynamic-slice.55) | copy-start | bytes 94
  1151.7 24.0 %collective-permute-start.18 = (bf16[16,2560]{1,0:T(8,128)(2,1)}, bf16[16,2560]{1,0:T(8,128)(2,1)S(1)}, u32[]{:S(2)}, u32[]{:S(2)}) collective-permute-start(bf16[16,2560]{1,0:T(8,128)(2,1)} %convert.70), channel_id=1, source_target_pairs={{0,3},{1,4},{2,5},{3,6},{4,7},{5,8},{6,9},{7,10},{8,11},{9,12},{10... | collective-permute-start | bytes 245768
  1153.5 32.1 %collective-permute-start.16 = (bf16[16,2560]{1,0:T(8,128)(2,1)}, bf16[16,2560]{1,0:T(8,128)(2,1)}, u32[]{:S(2)}, u32[]{:S(2)}) collective-permute-start(bf16[16,2560]{1,0:T(8,128)(2,1)} %convert.70), channel_id=1, source_target_pairs={{0,1},{1,2},{2,3},{3,4},{4,5},{5,6},{6,7},{7,8},{8,9},{9,10},{10,1... | collective-permute-start | bytes 245768
  1158.5 9.5 collective-permute-start.19
  1165.2 23.1 %collective-permute-start.13 = (bf16[16,2560]{1,0:T(8,128)(2,1)}, bf16[16,2560]{1,0:T(8,128)(2,1)S(1)}, u32[]{:S(2)}, u32[]{:S(2)}) collective-permute-start(bf16[16,2560]{1,0:T(8,128)(2,1)} %convert.71), channel_id=1, source_target_pairs={{0,2},{1,3},{2,4},{3,5},{4,6},{5,7},{6,8},{7,9},{8,10},{9,11},{10,... | collective-permute-start | bytes 245768
  1168.0 20.3 %collective-permute-start.14 = (bf16[16,2560]{1,0:T(8,128)(2,1)}, bf16[16,2560]{1,0:T(8,128)(2,1)S(1)}, u32[]{:S(2)}, u32[]{:S(2)}) collective-permute-start(bf16[16,2560]{1,0:T(8,128)(2,1)} %convert.71), channel_id=1, source_target_pairs={{0,3},{1,4},{2,5},{3,6},{4,7},{5,8},{6,9},{7,10},{8,11},{9,12},{10... | collective-permute-start | bytes 245768
  1169.9 18.4 %collective-permute-start.12 = (bf16[16,2560]{1,0:T(8,128)(2,1)}, bf16[16,2560]{1,0:T(8,128)(2,1)S(1)}, u32[]{:S(2)}, u32[]{:S(2)}) collective-permute-start(bf16[16,2560]{1,0:T(8,128)(2,1)} %convert.71), channel_id=1, source_target_pairs={{0,1},{1,2},{2,3},{3,4},{4,5},{5,6},{6,7},{7,8},{8,9},{9,10},{10,1... | collective-permute-start | bytes 245768
  1175.7 12.6 %collective-permute-start.15 = (bf16[15,2560]{1,0:T(8,128)(2,1)}, bf16[15,2560]{1,0:T(8,128)(2,1)S(1)}, u32[]{:S(2)}, u32[]{:S(2)}) collective-permute-start(bf16[15,2560]{1,0:T(8,128)(2,1)} %slice.154), channel_id=1, source_target_pairs={{0,4},{1,5},{2,6},{3,7},{4,8},{5,9},{6,10},{7,11},{8,12},{9,13},{1... | collective-permute-start | bytes 230408
  (39 other events, 203.2 us)
Sparse Core Ops, SparseCore 0:
  11.7 123.1 all-gather.2
  1199.2 33.0 all-reduce.19
where the time goes:
time: 1260 us; the launch traced here: 1250 us
  blocking collectives  629 us (50%)
  matrix products  215 us (17%)
  waiting for transfers between devices  145 us (12%)
  local copies, waits for them, and re-layouts  106 us (8%)
  starting transfers between devices  90.1 us (7%)
  other arithmetic  47.5 us (4%)
  between operations  17.1 us (1%)
    unnamed x2, blocking collectives  629 us
    all_gather x1, waiting for transfers between devices, gather_turned(): lax.all_gather(both, axis, axis=0, tiled=True)  118 us
    unnamed x28, starting transfers between devices  90 us
    dot_general x7, matrix products, contract_product(): lax.dot_general(left, weight, (((1,), (1,)), ((), ())), preferred_element...  52.3 us
    unnamed x102, local copies, waits for them, and re-layouts  38.9 us
    dot_general x7, matrix products, tdot(): lax.dot_general(left, right, (((0,), (0,)), ((), ())), preferred_element_...  36.5 us
    psum x1, waiting for transfers between devices, packed_total(): so_far = lax.psum(vector, axis)  27 us
  transfers between devices with their start and end apart: 30, of which 2 were waited for; matrix products, arithmetic and copies ran while one was open for 2% of the time, Pallas kernels for 0%

commit v1 on v0

--- a/solution.py
+++ b/solution.py
@@ -15,7 +15,13 @@
 def gather_turned(arrays, axis, dims):
     turned = [jnp.moveaxis(a, dim, 0) for a, dim in zip(arrays, dims)]
     both = jnp.concatenate([t.reshape(len(t), -1) for t in turned], axis=1)
-    whole, at, finished = (lax.all_gather(both, axis, axis=0, tiled=True), 0, [])
+    whole, at, finished = (
+        jnp.concatenate(
+            lax.all_to_all(jnp.stack([both] * lax.axis_size(axis)), axis, 0, 0), axis=0
+        ),
+        0,
+        [],
+    )
     for t, dim in zip(turned, dims):
         section = whole[:, at : at + t[0].size].reshape(-1, *t.shape[1:])
         finished.append(jnp.moveaxis(section, 0, dim))

time: 1260 us -> 1480 us (1.17)
  waiting for transfers between devices: 145 us -> 328 us
  blocking collectives: 629 us -> 651 us
    all_to_all x0 -> x1, waiting for transfers between devices: none -> 301 us  [gather_turned(): lax.all_to_all(jnp.stack([both] * lax.axis_size(axis)), axis, 0, 0)]
    all_gather x1 -> x0, waiting for transfers between devices: 118 us -> none  [gather_turned(): lax.all_gather(both, axis, axis=0, tiled=True)]
    unnamed x2, blocking collectives: 629 us -> 651 us
    unnamed x102 -> x103, local copies, waits for them, and re-layouts: 38.9 us -> 18.1 us
    reshape x0 -> x1, local copies, waits for them, and re-layouts: none -> 20.1 us  [gather_turned(): jnp.concatenate(lax.all_to_all(jnp.stack([both] * lax.axis_size(axis)), a...]
where the time goes in v1:
time: 1480 us; the launch traced here: 1470 us
  blocking collectives  651 us (44%)
  waiting for transfers between devices  328 us (22%)
  matrix products  215 us (15%)
  local copies, waits for them, and re-layouts  112 us (8%)
  starting transfers between devices  98.5 us (7%)
  other arithmetic  45.8 us (3%)
  between operations  17.1 us (1%)
    unnamed x2, blocking collectives  651 us
    all_to_all x1, waiting for transfers between devices, gather_turned(): lax.all_to_all(jnp.stack([both] * lax.axis_size(axis)), axis, 0, 0)  301 us
    unnamed x28, starting transfers between devices  85.8 us
    dot_general x7, matrix products, contract_product(): lax.dot_general(left, weight, (((1,), (1,)), ((), ())), preferred_element...  52.3 us
    dot_general x7, matrix products, tdot(): lax.dot_general(left, right, (((0,), (0,)), ((), ())), preferred_element_...  36.5 us
  transfers between devices with their start and end apart: 30, of which 2 were waited for; matrix products, arithmetic and copies ran while one was open for 2% of the time, Pallas kernels for 0%

profile of v1, /device:TPU:1, one launch (start us, length us, event | category | flops | bytes accessed | tf_op | source)
XLA Modules:
  0.0 1468.0 jit_solution(24826479735629516)
XLA Ops:
  9.9 7.3 stack.2
  17.2 12.6 all-to-all-start
  33.3 300.8 %all-to-all-done = bf16[64,15,10242]{2,1,0:T(8,128)(2,1)} async-done(((bf16[64,15,10242]{2,1,0:T(8,128)(2,1)}), bf16[64,15,10242]{2,1,0:T(8,128)(2,1)}, u32[]{:S(2)}, u32[]{:S(2)}) %all-to-all-start) | async-done | bytes 19664672 | tf_op jit(solution)/shard_map/all_to_all | solution.py:20
  334.1 20.1 %reshape.286 = bf16[960,10242]{1,0:T(8,128)(2,1)} reshape(bf16[64,15,10242]{2,1,0:T(8,128)(2,1)} %all-to-all-done) | data formatting | bytes 39329280 | tf_op jit(solution)/shard_map/reshape | solution.py:19
  361.4 5.8 fusion.99
  371.5 6.4 reshape.289
  384.1 50.4 %while.26 = (s32[]{:T(128)}, bf16[2,512,5,3,64]{1,4,3,2,0:T(8,128)(2,1)}, f32[2,5,3,512]{3,2,1,0:T(4,128)}, bf16[2,512,5,64]{1,3,2,0:T(8,128)(2,1)S(1)}, bf16[2,...) while((s32[]{:T(128)}, bf16[2,512,5,3,64]{1,4,3,2,0:T(8,128)(2,1)}, ...), condition=%wide.region_4.5_spmd, body=%wide.region_1.4_spmd.sunk | while | flops 1050632704 | bytes 67375304 | solution.py:160
  384.2 6.9 fusion.180
  391.2 8.9 exponential_reduce_fusion.2
  400.1 7.8 fusion.181
  409.3 6.9 fusion.180
  416.2 8.9 exponential_reduce_fusion.2
  425.1 7.8 fusion.181
  438.9 4.6 multiply_reduce_fusion.2
  445.8 11.7 fusion.78
  457.6 10.7 fusion.68
  468.2 19.1 %fusion.65 = (bf16[1024,2560]{1,0:T(8,128)(2,1)}, bf16[1024,2560]{1,0:T(8,128)(2,1)}, bf16[1024,2560]{1,0:T(8,128)(2,1)}) fusion(f32[2560,1024]{0,1:T(8,128)} %fusion.68, f32[1024,2560]{1,0:T(8,128)} %fusion.78, bf16[1024,960]{0,1:T(8,128)(2,1)} %copy-done.23, bf16[960,10242]{1,0:T(8,128)(2,1)} %reshape.286), kind=kOutput, calls=%fused_computation.68 | convolution fusion | flops 5075107840 | bytes 43581440 | tf_op jit(solution)/shard_map/dot_general | solution.py:166
  487.4 9.1 fusion.72
  496.5 9.1 multiply_reduce_fusion
  511.5 5.7 convolution_convert_fusion
  517.2 6.2 reshape.291
  526.7 59.5 %while.27 = (s32[]{:T(128)}, f32[2,512,5,3,64]{1,4,3,2,0:T(8,128)}, f32[2,512,5,64]{1,3,2,0:T(8,128)}, bf16[2,512,5,64]{1,3,2,0:T(8,128)(2,1)}, bf16[2,512,5,64]...) while((s32[]{:T(128)}, f32[2,512,5,3,64]{1,4,3,2,0:T(8,128)}, ...), condition=%wide.region_9.10_spmd, body=%wide.region_7.9_spmd.sunk | while | flops 2558779904 | bytes 186770704 | solution.py:279
  530.9 5.4 copy-done
  536.3 5.6 fusion.196
  541.9 8.6 fusion.194
  560.6 5.4 copy-done
  566.0 5.6 fusion.196
  571.5 8.6 fusion.194
  592.7 4.6 fusion.110
  606.1 5.8 fusion.97
  612.0 8.0 fusion.136
  620.0 7.7 fusion.137
  627.7 9.0 add_convert_fusion
  636.7 7.8 fusion.138
  647.6 476.8 %fusion.127 = (f32[16,960]{1,0:T(8,128)S(1)}, f32[16,320]{1,0:T(8,128)S(1)}, f32[16,320]{1,0:T(8,128)S(1)}, f32[16,2560]{1,0:T(8,128)S(1)}, f32[16,2560]{1,0:T(8...) fusion(f32[960,960]{1,0:T(8,128)} %fusion.122, f32[960,320]{1,0:T(8,128)} %fusion.120, ...), kind=kCustom, calls=%all-reduce-scatter.7 | all-reduce-scatter fusion | flops 10485761 | bytes 39977472
  1132.1 7.2 fusion.87
  1142.6 173.9 %all-reduce.16 = (bf16[960]{0:T(1024)(128)(2,1)S(1)}, bf16[960]{0:T(1024)(128)(2,1)S(1)}) all-reduce(f32[960]{0:T(1024)S(1)} %get-tuple-element.177, f32[960]{0:T(1024)S(1)} %copy-done.38), channel_id=9, replica_groups=mesh['replica'=2,'shard'=64] {'shard'}, use_global_device_ids=true, to_apply=%region_19.20.clone | all-reduce | flops 1920 | bytes 11520
  1325.5 5.8 collective-permute-start.2
  1334.5 4.6 collective-permute-start.21
  1347.1 4.7 collective-permute-start.25
  1355.0 4.4 collective-permute-start.24
  1370.4 5.0 collective-permute-start.16
  1375.4 5.7 collective-permute-start.19
  1385.8 5.8 collective-permute-start.12
  1391.6 11.1 collective-permute-start.15
  1407.8 8.3 concatenate.45
  1416.2 6.2 fusion.84
  1422.4 27.2 %all-reduce.20.cloned.1.call-done = bf16[153630]{0:T(1024)(128)(2,1)} async-done(((bf16[153630]{0:T(1024)(128)(2,1)}), bf16[153630]{0:T(1024)(128)(2,1)}) %all-reduce.20.cloned.1.call-update) | async-done | bytes 307276 | tf_op jit(solution)/shard_map/psum | solution.py:34
  (283 shorter events, 145.0 us)
Async XLA Ops:
  17.2 12.7 copy-start.39
  17.2 15.0 %copy-start.4 = (bf16[1024,960]{0,1:T(8,128)(2,1)S(1)}, bf16[1024,960]{0,1:T(8,128)(2,1)}, u32[]{:S(2)}) copy-start(bf16[1024,960]{0,1:T(8,128)(2,1)} %param.15) | copy-start | bytes 5898244
  17.2 316.9 %all-to-all-start = ((bf16[64,15,10242]{2,1,0:T(8,128)(2,1)}), bf16[64,15,10242]{2,1,0:T(8,128)(2,1)}, u32[]{:S(2)}, u32[]{:S(2)}) async-start(bf16[64,15,10242]{2,1,0:T(8,128)(2,1)} %stack.2), calls=%async_computation | async-start | bytes 42467328 | tf_op jit(solution)/shard_map/all_to_all | solution.py:20
  29.8 1419.7 %all-reduce.20.cloned.1.call-start = ((), (), s32[]{:S(2)}) async-start(), calls=%async_computation.1 | async-start | bytes 618496 | tf_op jit(solution)/shard_map/psum | solution.py:34
  32.2 349.6 %copy-start.16 = (f32[512,64]{0,1:T(8,128)}, f32[512,64]{0,1:T(8,128)S(1)}, u32[]{:S(2)}) copy-start(f32[512,64]{0,1:T(8,128)S(1)} %get-tuple-element.266) | copy-start | bytes 393220
  32.2 349.5 %copy-start.18 = (f32[512,64]{0,1:T(8,128)}, f32[512,64]{0,1:T(8,128)S(1)}, u32[]{:S(2)}) copy-start(f32[512,64]{0,1:T(8,128)S(1)} %get-tuple-element.267) | copy-start | bytes 393220
  33.3 328.1 %copy-start.35 = (f32[1024]{0:T(1024)}, f32[1024]{0:T(1024)S(1)}, u32[]{:S(2)}) copy-start(f32[1024]{0:T(1024)S(1)} %get-tuple-element.275) | copy-start | bytes 12292
  445.8 11.7 copy-start.23
  445.8 11.7 copy-start.20
  517.2 9.4 copy-start.31
  526.6 61.2 %copy-start.17 = (f32[512,64]{0,1:T(8,128)S(1)}, f32[512,64]{0,1:T(8,128)}, u32[]{:S(2)}) copy-start(f32[512,64]{0,1:T(8,128)} %copy-done.16) | copy-start | bytes 393220
  526.6 61.2 %copy-start.19 = (f32[512,64]{0,1:T(8,128)S(1)}, f32[512,64]{0,1:T(8,128)}, u32[]{:S(2)}) copy-start(f32[512,64]{0,1:T(8,128)} %copy-done.18) | copy-start | bytes 393220
  601.4 10.5 slice-start.4
  601.9 10.0 slice-start.5
  606.1 13.8 slice-start.2
  612.0 15.7 %slice-start = ((s8[5242880]{0:T(1024)(128)(4,1)}), s8[4194304]{0:T(1024)(128)(4,1)S(1)}, s32[]{:S(2)}) async-start(s8[5242880]{0:T(1024)(128)(4,1)} %bitcast.276), calls=%async_computation.2 | async-start | bytes 8388608
  1124.5 18.1 %copy-start.38 = (f32[960]{0:T(1024)S(1)}, f32[960]{0:T(1024)}, u32[]{:S(2)}) copy-start(f32[960]{0:T(1024)} %get-tuple-element.175) | copy-start | bytes 11524
  1124.5 195.8 %collective-permute-start.9 = (bf16[16,320]{1,0:T(8,128)(2,1)S(1)}, bf16[16,320]{1,0:T(8,128)(2,1)S(1)}, u32[]{:S(2)}, u32[]{:S(2)}) collective-permute-start(bf16[16,320]{1,0:T(8,128)(2,1)S(1)} %convert.74), channel_id=1, source_target_pairs={{0,2},{1,3},{2,4},{3,5},{4,6},{5,7},{6,8},{7,9},{8,10},{9,11},{10,... | collective-permute-start | bytes 30728
  1125.8 196.4 %collective-permute-start.10 = (bf16[16,320]{1,0:T(8,128)(2,1)S(1)}, bf16[16,320]{1,0:T(8,128)(2,1)S(1)}, u32[]{:S(2)}, u32[]{:S(2)}) collective-permute-start(bf16[16,320]{1,0:T(8,128)(2,1)S(1)} %convert.74), channel_id=1, source_target_pairs={{0,3},{1,4},{2,5},{3,6},{4,7},{5,8},{6,9},{7,10},{8,11},{9,12},{10... | collective-permute-start | bytes 30728
  1128.5 195.0 %collective-permute-start.8 = (bf16[16,320]{1,0:T(8,128)(2,1)S(1)}, bf16[16,320]{1,0:T(8,128)(2,1)S(1)}, u32[]{:S(2)}, u32[]{:S(2)}) collective-permute-start(bf16[16,320]{1,0:T(8,128)(2,1)S(1)} %convert.74), channel_id=1, source_target_pairs={{0,1},{1,2},{2,3},{3,4},{4,5},{5,6},{6,7},{7,8},{8,9},{9,10},{10,1... | collective-permute-start | bytes 30728
  1130.4 188.5 %collective-permute-start.11 = (bf16[15,320]{1,0:T(8,128)(2,1)S(1)}, bf16[15,320]{1,0:T(8,128)(2,1)S(1)}, u32[]{:S(2)}, u32[]{:S(2)}) collective-permute-start(bf16[15,320]{1,0:T(8,128)(2,1)S(1)} %slice.153), channel_id=1, source_target_pairs={{0,4},{1,5},{2,6},{3,7},{4,8},{5,9},{6,10},{7,11},{8,12},{9,13},{1... | collective-permute-start | bytes 28808
  1317.6 13.6 collective-permute-start.5
  1318.9 14.3 collective-permute-start.6
  1320.2 14.3 collective-permute-start.4
  1322.2 3.3 collective-permute-start.7
  1323.5 18.4 %collective-permute-start.1 = (bf16[16,960]{1,0:T(8,128)(2,1)S(1)}, bf16[16,960]{1,0:T(8,128)(2,1)S(1)}, u32[]{:S(2)}, u32[]{:S(2)}) collective-permute-start(bf16[16,960]{1,0:T(8,128)(2,1)S(1)} %convert.73), channel_id=1, source_target_pairs={{0,2},{1,3},{2,4},{3,5},{4,6},{5,7},{6,8},{7,9},{8,10},{9,11},{10,... | collective-permute-start | bytes 92168
  1325.5 20.3 %collective-permute-start.2 = (bf16[16,960]{1,0:T(8,128)(2,1)S(1)}, bf16[16,960]{1,0:T(8,128)(2,1)S(1)}, u32[]{:S(2)}, u32[]{:S(2)}) collective-permute-start(bf16[16,960]{1,0:T(8,128)(2,1)S(1)} %convert.73), channel_id=1, source_target_pairs={{0,3},{1,4},{2,5},{3,6},{4,7},{5,8},{6,9},{7,10},{8,11},{9,12},{10... | collective-permute-start | bytes 92168
  1331.3 15.8 %collective-permute-start = (bf16[16,960]{1,0:T(8,128)(2,1)S(1)}, bf16[16,960]{1,0:T(8,128)(2,1)S(1)}, u32[]{:S(2)}, u32[]{:S(2)}) collective-permute-start(bf16[16,960]{1,0:T(8,128)(2,1)S(1)} %convert.73), channel_id=1, source_target_pairs={{0,1},{1,2},{2,3},{3,4},{4,5},{5,6},{6,7},{7,8},{8,9},{9,10},{10,1... | collective-permute-start | bytes 92168
  1333.2 7.4 collective-permute-start.3
  1334.5 20.5 %collective-permute-start.21 = (bf16[960,16]{0,1:T(8,128)(2,1)S(1)}, bf16[960,16]{0,1:T(8,128)(2,1)S(1)}, u32[]{:S(2)}, u32[]{:S(2)}) collective-permute-start(bf16[960,16]{0,1:T(8,128)(2,1)S(1)} %convert.72), channel_id=1, source_target_pairs={{0,2},{1,3},{2,4},{3,5},{4,6},{5,7},{6,8},{7,9},{8,10},{9,11},{10,... | collective-permute-start | bytes 92168
  1340.6 18.8 %collective-permute-start.22 = (bf16[960,16]{0,1:T(8,128)(2,1)S(1)}, bf16[960,16]{0,1:T(8,128)(2,1)S(1)}, u32[]{:S(2)}, u32[]{:S(2)}) collective-permute-start(bf16[960,16]{0,1:T(8,128)(2,1)S(1)} %convert.72), channel_id=1, source_target_pairs={{0,3},{1,4},{2,5},{3,6},{4,7},{5,8},{6,9},{7,10},{8,11},{9,12},{10... | collective-permute-start | bytes 92168
  1341.9 20.9 %collective-permute-start.20 = (bf16[960,16]{0,1:T(8,128)(2,1)S(1)}, bf16[960,16]{0,1:T(8,128)(2,1)}, u32[]{:S(2)}, u32[]{:S(2)}) collective-permute-start(bf16[960,16]{0,1:T(8,128)(2,1)S(1)} %convert.72), channel_id=1, source_target_pairs={{0,1},{1,2},{2,3},{3,4},{4,5},{5,6},{6,7},{7,8},{8,9},{9,10},{10,1... | collective-permute-start | bytes 92168
  1345.8 6.7 collective-permute-start.23
  1347.1 23.3 %collective-permute-start.25 = (bf16[2560,16]{0,1:T(8,128)(2,1)S(1)}, bf16[2560,16]{0,1:T(8,128)(2,1)S(1)}, u32[]{:S(2)}, u32[]{:S(2)}) collective-permute-start(bf16[2560,16]{0,1:T(8,128)(2,1)S(1)} %convert.69), channel_id=1, source_target_pairs={{0,2},{1,3},{2,4},{3,5},{4,6},{5,7},{6,8},{7,9},{8,10},{9,11},{10,... | collective-permute-start | bytes 245768
  1352.5 22.9 %collective-permute-start.26 = (bf16[2560,16]{0,1:T(8,128)(2,1)S(1)}, bf16[2560,16]{0,1:T(8,128)(2,1)S(1)}, u32[]{:S(2)}, u32[]{:S(2)}) collective-permute-start(bf16[2560,16]{0,1:T(8,128)(2,1)S(1)} %convert.69), channel_id=1, source_target_pairs={{0,3},{1,4},{2,5},{3,6},{4,7},{5,8},{6,9},{7,10},{8,11},{9,12},{10... | collective-permute-start | bytes 245768
  1355.0 26.1 %collective-permute-start.24 = (bf16[2560,16]{0,1:T(8,128)(2,1)S(1)}, bf16[2560,16]{0,1:T(8,128)(2,1)S(1)}, u32[]{:S(2)}, u32[]{:S(2)}) collective-permute-start(bf16[2560,16]{0,1:T(8,128)(2,1)S(1)} %convert.69), channel_id=1, source_target_pairs={{0,1},{1,2},{2,3},{3,4},{4,5},{5,6},{6,7},{7,8},{8,9},{9,10},{10,1... | collective-permute-start | bytes 245768
  1359.4 9.2 collective-permute-start.27
  1362.7 23.1 %collective-permute-start.17 = (bf16[16,2560]{1,0:T(8,128)(2,1)}, bf16[16,2560]{1,0:T(8,128)(2,1)S(1)}, u32[]{:S(2)}, u32[]{:S(2)}) collective-permute-start(bf16[16,2560]{1,0:T(8,128)(2,1)} %convert.70), channel_id=1, source_target_pairs={{0,2},{1,3},{2,4},{3,5},{4,6},{5,7},{6,8},{7,9},{8,10},{9,11},{10,... | collective-permute-start | bytes 245768
  1367.9 39.9 %copy-start.32 = (bf16[4800]{0:T(1024)(128)(2,1)S(1)}, bf16[4800]{0:T(1024)(128)(2,1)}, u32[]{:S(2)}) copy-start(bf16[4800]{0:T(1024)(128)(2,1)} %reshape.296) | copy-start | bytes 28804
  1367.9 39.9 %copy-start.40 = (bf16[15]{0:T(256)(128)(2,1)S(1)}, bf16[15]{0:T(256)(128)(2,1)}, u32[]{:S(2)}) copy-start(bf16[15]{0:T(256)(128)(2,1)} %dynamic-slice.56) | copy-start | bytes 94
  1368.0 39.9 %copy-start.41 = (bf16[15]{0:T(256)(128)(2,1)S(1)}, bf16[15]{0:T(256)(128)(2,1)}, u32[]{:S(2)}) copy-start(bf16[15]{0:T(256)(128)(2,1)} %dynamic-slice.55) | copy-start | bytes 94
  1368.6 23.0 %collective-permute-start.18 = (bf16[16,2560]{1,0:T(8,128)(2,1)}, bf16[16,2560]{1,0:T(8,128)(2,1)S(1)}, u32[]{:S(2)}, u32[]{:S(2)}) collective-permute-start(bf16[16,2560]{1,0:T(8,128)(2,1)} %convert.70), channel_id=1, source_target_pairs={{0,3},{1,4},{2,5},{3,6},{4,7},{5,8},{6,9},{7,10},{8,11},{9,12},{10... | collective-permute-start | bytes 245768
  1370.4 32.3 %collective-permute-start.16 = (bf16[16,2560]{1,0:T(8,128)(2,1)}, bf16[16,2560]{1,0:T(8,128)(2,1)}, u32[]{:S(2)}, u32[]{:S(2)}) collective-permute-start(bf16[16,2560]{1,0:T(8,128)(2,1)} %convert.70), channel_id=1, source_target_pairs={{0,1},{1,2},{2,3},{3,4},{4,5},{5,6},{6,7},{7,8},{8,9},{9,10},{10,1... | collective-permute-start | bytes 245768
  1375.4 8.6 collective-permute-start.19
  1381.1 24.3 %collective-permute-start.13 = (bf16[16,2560]{1,0:T(8,128)(2,1)}, bf16[16,2560]{1,0:T(8,128)(2,1)S(1)}, u32[]{:S(2)}, u32[]{:S(2)}) collective-permute-start(bf16[16,2560]{1,0:T(8,128)(2,1)} %convert.71), channel_id=1, source_target_pairs={{0,2},{1,3},{2,4},{3,5},{4,6},{5,7},{6,8},{7,9},{8,10},{9,11},{10,... | collective-permute-start | bytes 245768
  1384.0 21.5 %collective-permute-start.14 = (bf16[16,2560]{1,0:T(8,128)(2,1)}, bf16[16,2560]{1,0:T(8,128)(2,1)S(1)}, u32[]{:S(2)}, u32[]{:S(2)}) collective-permute-start(bf16[16,2560]{1,0:T(8,128)(2,1)} %convert.71), channel_id=1, source_target_pairs={{0,3},{1,4},{2,5},{3,6},{4,7},{5,8},{6,9},{7,10},{8,11},{9,12},{10... | collective-permute-start | bytes 245768
  1385.8 19.6 %collective-permute-start.12 = (bf16[16,2560]{1,0:T(8,128)(2,1)}, bf16[16,2560]{1,0:T(8,128)(2,1)S(1)}, u32[]{:S(2)}, u32[]{:S(2)}) collective-permute-start(bf16[16,2560]{1,0:T(8,128)(2,1)} %convert.71), channel_id=1, source_target_pairs={{0,1},{1,2},{2,3},{3,4},{4,5},{5,6},{6,7},{7,8},{8,9},{9,10},{10,1... | collective-permute-start | bytes 245768
  1391.6 13.8 collective-permute-start.15
  (40 other events, 212.4 us)
Sparse Core Ops, SparseCore 0:
  1416.3 33.1 all-reduce.19
